TPU v7x, 512 devices: a whole 4x4x16 slice. The times are simulated.
512 devices in a mesh: req: 32 (over y, x, core), tok: 16 (over z).
Axes of the slice: x: 4, y: 4, z: 16, core: 2. Of those that a mesh axis runs over, the one named last changes fastest.
Arguments:
- queries: bfloat16 [128, 4, 128, 1024], P('req', None, 'tok'), may hold values from -18 to 18
- keys: bfloat16 [128, 4, 128, 128], P('req', None, 'tok'), may hold values from -5 to 5
- values: bfloat16 [128, 4, 128, 128], P('req', None, 'tok'), may hold values from -4 to 4
- key_cache_pool: bfloat16 [2048, 128, 2048], P('req', None, 'tok'), may hold values from -4 to 4
- value_cache_pool: bfloat16 [2048, 128, 2048], P('req', None, 'tok'), may hold values from -4 to 4
- cached_len: int32 [128], replicated, may hold values from 3072 to 4096, as said below
- page_table: int32 [128, 32, 2], replicated, may hold values from 0 to 63, as said below
Outputs:
- attended: bfloat16 [128, 4, 128, 1024], P('req', None, 'tok')
- new_keys: bfloat16 [128, 4, 128, 128], P('req', None, 'tok')
Inputs may be any that keep to these rules, and one draw needn't show every extreme that they name: `cached_len`: A whole number of pages. In every draw some request whose pages lie in other groups has 32 pages. `page_table`: exactly half of the requests keep all pages in their own group, in slots below 32; for each other request of group g, page p lies in group (g + 1 + p) mod 32 in a slot of 32 or more. No two live pages of requests of one lane share a group and slot. So at most 1 pages of one request lie in one other group, and every draw reaches it. Entries past a request's pages are not used.
All inputs are finite; a program needn't handle non-finite values.
Results may differ from a plain program's by a relative error of at most 0.008.
Values may be sent and summed in bfloat16 or wider, within the bound.
A program may use at most 64 MiB of HBM per device.

v0:
```python
import jax
import jax.numpy as jnp
from jax import lax
from jax.sharding import PartitionSpec as P

THETA = 5000000.0
NEGATIVE = -1e30
FAR_AWAY = 1 << 30


def apply_rotary(vectors, token_positions):
    head_dim = vectors.shape[-1]
    half_dim = head_dim // 2
    inverse = THETA ** (-(jnp.arange(half_dim, dtype=jnp.float32) * 2.0 / head_dim))
    angles = token_positions.astype(jnp.float32)[..., None] * inverse
    cosine = jnp.cos(angles)
    sine_table = jnp.sin(angles)
    first_half = vectors[..., :half_dim]
    back_half = vectors[..., half_dim:]
    return jnp.concatenate(
        [
            first_half * cosine - back_half * sine_table,
            back_half * cosine + first_half * sine_table,
        ],
        axis=-1,
    )


def ranked(held_mask, slot_ids, capacity):
    order_rank = jnp.cumsum(held_mask.astype(jnp.int32), axis=-1) - 1
    capacity_slots = jnp.arange(capacity, dtype=jnp.int32)
    chosen = held_mask[..., None, :] & (order_rank[..., None, :] == capacity_slots[:, None])
    selected_rows = jnp.sum(jnp.where(chosen, slot_ids[..., None, :], 0), axis=-1)
    return (selected_rows, jnp.any(chosen, axis=-1))


def pick_one(stacked, lane_index, head_index):
    lane_rows = lax.dynamic_index_in_dim(stacked, lane_index, 0, False)
    return lax.dynamic_index_in_dim(lane_rows, head_index, 0, False)


def compacted(page_keys, page_values, key_place, live, block_pages):
    page_total = page_keys.shape[0]
    padding = -(-page_total // block_pages) * block_pages - page_total
    page_keys = jnp.concatenate(
        [page_keys, jnp.zeros((padding,) + page_keys.shape[1:], page_keys.dtype)]
    )
    page_values = jnp.concatenate(
        [page_values, jnp.zeros((padding,) + page_values.shape[1:], page_values.dtype)]
    )
    key_place = jnp.concatenate(
        [key_place, jnp.full((padding, key_place.shape[1]), FAR_AWAY, jnp.int32)]
    )
    live = jnp.concatenate([live, jnp.zeros((padding,), bool)])
    arrangement = jnp.argsort(jnp.logical_not(live).astype(jnp.int32), stable=True)
    block_count = (jnp.sum(live.astype(jnp.int32)) + block_pages - 1) // block_pages
    return (page_keys[arrangement], page_values[arrangement], key_place[arrangement], block_count)


def block_scores(rotated, key_pages, key_place, block_number, block_pages, score_scale):
    head_dim = key_pages.shape[-1]
    block_keys = block_pages * key_pages.shape[1]
    key_block = lax.dynamic_slice_in_dim(
        key_pages, block_number * block_pages, block_pages, 0
    ).reshape(block_keys, head_dim)
    place_block = lax.dynamic_slice_in_dim(
        key_place, block_number * block_pages, block_pages, 0
    ).reshape(block_keys)
    scores = (
        jnp.einsum("qgd,kd->qgk", rotated, key_block, preferred_element_type=jnp.float32)
        * score_scale
    )
    return (scores, place_block)


def highest_scores(rotated, token_index, key_set, block_pages, score_scale, start_high):
    key_pages, value_pages, key_place, block_count = key_set

    def highest_one_block(block_number, highest):
        scores, place_block = block_scores(
            rotated, key_pages, key_place, block_number, block_pages, score_scale
        )
        visible = place_block[None, None, :] <= token_index[:, None, None]
        return jnp.maximum(highest, jnp.max(jnp.where(visible, scores, NEGATIVE), axis=-1))

    return lax.fori_loop(0, block_count, highest_one_block, start_high)


def weighted_sums(rotated, token_index, key_set, block_pages, score_scale, row_max, start_sums):
    key_pages, value_pages, key_place, block_count = key_set
    head_dim = key_pages.shape[-1]
    block_keys = block_pages * key_pages.shape[1]

    def weighted_one_block(block_number, carried):
        value_sum, total_weight = carried
        scores, place_block = block_scores(
            rotated, key_pages, key_place, block_number, block_pages, score_scale
        )
        value_block = lax.dynamic_slice_in_dim(
            value_pages, block_number * block_pages, block_pages, 0
        ).reshape(block_keys, head_dim)
        visible = place_block[None, None, :] <= token_index[:, None, None]
        weights = jnp.where(visible, jnp.exp(scores - row_max[..., None]), 0.0)
        total_weight = total_weight + jnp.sum(weights, axis=-1)
        value_sum = value_sum + jnp.einsum(
            "qgk,kd->qgd",
            weights.astype(jnp.bfloat16),
            value_block,
            preferred_element_type=jnp.float32,
        )
        return (value_sum, total_weight)

    return lax.fori_loop(0, block_count, weighted_one_block, start_sums)


def per_device(queries, keys, values, key_cache_pool, value_cache_pool, cached_len, page_table):
    group_count = lax.axis_size("req")
    member_count = lax.axis_size("tok")
    group_index = lax.axis_index("req")
    member_index = lax.axis_index("tok")
    lane_count, kv_count, token_slice, query_width = queries.shape
    head_dim = keys.shape[-1]
    heads_per_group = query_width // head_dim
    added_rows = token_slice * member_count
    page_rows = key_cache_pool.shape[1]
    page_limit = page_table.shape[1]
    capacity = (page_limit + group_count - 1) // group_count
    block_pages = max(1, 512 // page_rows)
    score_scale = head_dim ** (-0.5)
    lane_index = member_index // kv_count
    head_index = member_index % kv_count
    own_request = group_index * lane_count + lane_index
    group_requests = group_index * lane_count + jnp.arange(lane_count, dtype=jnp.int32)
    offsets = member_index * token_slice + jnp.arange(token_slice, dtype=jnp.int32)
    token_positions = cached_len[group_requests][:, None] + offsets[None, :]
    query_rotated = apply_rotary(
        queries.astype(jnp.float32).reshape(
            lane_count, kv_count, token_slice, heads_per_group, head_dim
        ),
        token_positions[:, None, :, None],
    ).astype(jnp.bfloat16)
    new_keys = apply_rotary(keys.astype(jnp.float32), token_positions[:, None, :]).astype(
        jnp.bfloat16
    )
    own_queries = lax.all_to_all(
        query_rotated.reshape(member_count, token_slice, query_width),
        "tok",
        split_axis=0,
        concat_axis=1,
        tiled=True,
    )
    own_queries = own_queries.reshape(added_rows, heads_per_group, head_dim)
    every_keys, every_values = (
        lax.all_gather(new_keys, "tok", axis=2, tiled=True),
        lax.all_gather(values, "tok", axis=2, tiled=True),
    )
    fresh_key_rows = pick_one(every_keys, lane_index, head_index)
    fresh_value_rows = pick_one(every_values, lane_index, head_index)
    page_numbers = jnp.arange(page_limit, dtype=jnp.int32)
    group_numbers = jnp.arange(group_count, dtype=jnp.int32)
    lane_requests = group_numbers * lane_count + lane_index
    lane_table = page_table[lane_requests]
    lane_pages = cached_len[lane_requests] // page_rows
    held_mask = (
        (lane_table[:, :, 0] == group_index)
        & (page_numbers[None, :] < lane_pages[:, None])
        & (group_numbers[:, None] != group_index)
    )
    send_slots = ranked(held_mask, lane_table[:, :, 1], capacity)[0].reshape(-1)
    outgoing_keys = key_cache_pool[send_slots].reshape(group_count * capacity * page_rows, head_dim)
    outgoing_values = value_cache_pool[send_slots].reshape(
        group_count * capacity * page_rows, head_dim
    )
    incoming_keys, incoming_values = (
        lax.all_to_all(outgoing_keys, "req", split_axis=0, concat_axis=0, tiled=True),
        lax.all_to_all(outgoing_values, "req", split_axis=0, concat_axis=0, tiled=True),
    )
    own_table = page_table[own_request]
    own_live = page_numbers < cached_len[own_request] // page_rows
    own_holder = own_table[:, 0]
    at_home = own_live & (own_holder == group_index)
    elsewhere = (
        own_live[None, :]
        & (own_holder[None, :] == group_numbers[:, None])
        & (group_numbers[:, None] != group_index)
    )
    arrived = ranked(elsewhere, jnp.zeros((group_count, page_limit), jnp.int32), capacity)[
        1
    ].reshape(-1)
    home_keys = key_cache_pool[own_table[:, 1]]
    home_values = value_cache_pool[own_table[:, 1]]
    home_place = jnp.broadcast_to(
        jnp.where(at_home, -1, FAR_AWAY).astype(jnp.int32)[:, None], (page_limit, page_rows)
    )
    remote_place = jnp.broadcast_to(
        jnp.where(arrived, -1, FAR_AWAY).astype(jnp.int32)[:, None],
        (group_count * capacity, page_rows),
    )
    remote_keys = incoming_keys.reshape(group_count * capacity, page_rows, head_dim)
    remote_values = incoming_values.reshape(group_count * capacity, page_rows, head_dim)
    token_index = jnp.arange(added_rows, dtype=jnp.int32)
    fresh_pages = added_rows // page_rows
    fresh_keys_paged = fresh_key_rows.reshape(fresh_pages, page_rows, head_dim)
    fresh_values_paged = fresh_value_rows.reshape(fresh_pages, page_rows, head_dim)
    fresh_place = token_index.reshape(fresh_pages, page_rows)
    fresh_live = jnp.ones((fresh_pages,), bool)
    start_high = jnp.full((added_rows, heads_per_group), NEGATIVE, jnp.float32)
    start_sums = (
        jnp.zeros((added_rows, heads_per_group, head_dim), jnp.float32),
        jnp.zeros((added_rows, heads_per_group), jnp.float32),
    )
    joined = compacted(
        jnp.concatenate([fresh_keys_paged, home_keys, remote_keys]),
        jnp.concatenate([fresh_values_paged, home_values, remote_values]),
        jnp.concatenate([fresh_place, home_place, remote_place]),
        jnp.concatenate([fresh_live, at_home, arrived]),
        block_pages,
    )
    row_max = highest_scores(own_queries, token_index, joined, block_pages, score_scale, start_high)
    value_sum, total_weight = weighted_sums(
        own_queries, token_index, joined, block_pages, score_scale, row_max, start_sums
    )
    attended = (
        (value_sum / total_weight[..., None])
        .astype(jnp.bfloat16)
        .reshape(1, added_rows, query_width)
    )
    returned = lax.all_to_all(attended, "tok", split_axis=1, concat_axis=0, tiled=True)
    return (returned.reshape(lane_count, kv_count, token_slice, query_width), new_keys)


def solution(mesh):
    placed = (
        P("req", None, "tok", None),
        P("req", None, "tok", None),
        P("req", None, "tok", None),
        P("req", None, "tok"),
        P("req", None, "tok"),
        P(),
        P(),
    )
    return jax.shard_map(
        per_device,
        mesh=mesh,
        in_specs=placed,
        out_specs=(P("req", None, "tok", None), P("req", None, "tok", None)),
        check_vma=False,
    )
```

profile of v0, /device:TPU:44, one launch (start us, length us, event | category | flops | bytes accessed | tf_op | source)
XLA Modules:
  0.0 215.2 jit_solution(16100860536713558221)
XLA Ops:
  0.7 1.1 bitcast_convert_fusion
  1.9 1.3 gather_fusion.1
  3.6 0.9 pad_maximum_fusion
  4.5 15.2 %all-to-all-start.1 = ((bf16[16,8,1024]{2,1,0:T(8,128)(2,1)}), bf16[16,8,1024]{2,1,0:T(8,128)(2,1)S(1)}, u32[]{:S(2)}, u32[]{:S(2)}) async-start(bf16[16,8,1024]{2,1,0:T(8,128)(2,1)} %bitcast.14), calls=%async_computation.1 | async-start | bytes 524288 | tf_op jit(solution)/shard_map/all_to_all | solution.py:145
  25.9 1.7 gather_fusion.5
  27.6 10.0 %all-to-all-done.1 = bf16[16,8,1024]{2,1,0:T(8,128)(2,1)S(1)} async-done(((bf16[16,8,1024]{2,1,0:T(8,128)(2,1)}), bf16[16,8,1024]{2,1,0:T(8,128)(2,1)S(1)}, u32[]{:S(2)}, u32[]{:S(2)}) %all-to-all-start.1) | async-done | bytes 262176 | tf_op jit(solution)/shard_map/all_to_all | solution.py:145
  37.6 7.5 %all-to-all-start = ((bf16[32,128,128]{2,1,0:T(8,128)(2,1)}), bf16[32,128,128]{2,1,0:T(8,128)(2,1)}, u32[]{:S(2)}, u32[]{:S(2)}) async-start(bf16[32,128,128]{2,1,0:T(8,128)(2,1)} %gather_fusion.5), calls=%async_computation | async-start | bytes 2097152 | tf_op jit(solution)/shard_map/all_to_all | solution.py:175
  45.2 3.3 %gather_fusion.8 = bf16[32,128,128]{2,1,0:T(8,128)(2,1)} fusion(bf16[64,128,128]{2,1,0:T(8,128)(2,1)} %param.15, s32[1024]{0:T(1024)S(1)} %pad_clamp_fusion), kind=kCustom, calls=%fused_computation.8 | custom fusion | bytes 2097280 | tf_op jit(solution)/shard_map/gather | solution.py:171
  48.4 0.7 gather_fusion.2
  49.2 3.3 %gather_fusion.7 = bf16[32,128,128]{2,1,0:T(8,128)(2,1)} fusion(bf16[64,128,128]{2,1,0:T(8,128)(2,1)} %param.15, s32[1024]{0:T(1024)S(1)} %pad_clamp_fusion.2), kind=kCustom, calls=%fused_computation.7 | custom fusion | bytes 2097280 | tf_op jit(solution)/shard_map/gather | solution.py:191
  54.0 1.2 pad.13.clone
  55.9 2.6 %sort.17 = (s32[68]{0:T(128)}, s32[68]{0:T(128)S(1)}) sort(s32[68]{0:T(128)S(1)} %get-tuple-element.214, s32[68]{0:T(128)S(1)} %iota.62), dimensions={0}, to_apply=%region_5.6 | sort | flops 476 | bytes 1088 | tf_op jit(solution)/shard_map/jit(argsort)/sort | solution.py:55
  58.5 0.8 add_add_fusion
  59.3 1.2 gather_fusion
  60.5 7.4 %all-to-all-start.2 = ((bf16[32,128,128]{2,1,0:T(8,128)(2,1)}), bf16[32,128,128]{2,1,0:T(8,128)(2,1)}, u32[]{:S(2)}, u32[]{:S(2)}) async-start(bf16[32,128,128]{2,1,0:T(8,128)(2,1)} %gather_fusion.8), calls=%async_computation.2 | async-start | bytes 2097152 | tf_op jit(solution)/shard_map/all_to_all | solution.py:176
  68.1 29.6 %all_gather.6 = bf16[4,4,128,128]{3,2,1,0:T(8,128)(2,1)S(1)} all-gather(bf16[4,4,8,128]{3,2,1,0:T(8,128)(2,1)S(1)} %pad_maximum_fusion.1), channel_id=1, replica_groups=mesh['req'=32,'tok'=16] {'tok'}, dimensions={2}, use_global_device_ids=true | all-gather | bytes 557056 | tf_op jit(solution)/shard_map/all_gather | solution.py:154
  97.7 32.4 %all_gather.7 = bf16[4,4,128,128]{3,2,1,0:T(8,128)(2,1)S(1)} all-gather(bf16[4,4,8,128]{3,2,1,0:T(8,128)(2,1)} %param.13), channel_id=1, replica_groups=mesh['req'=32,'tok'=16] {'tok'}, dimensions={2}, use_global_device_ids=true | all-gather | bytes 557056 | tf_op jit(solution)/shard_map/all_gather | solution.py:155
  130.2 3.8 %maximum_maximum_fusion.1 = (bf16[68,128,128]{2,1,0:T(8,128)(2,1)}, bf16[68,128,128]{2,1,0:T(8,128)(2,1)}) fusion(bf16[32,128,128]{2,1,0:T(8,128)(2,1)} %all-to-all-done.2, bf16[32,128,128]{2,1,0:T(8,128)(2,1)} %gather_fusion.7, bf16[1,128,128]{2,1,0:T(8,128)(2,1)S(1)} %dynamic-slice_bitcast_fusion.2, bf16[68]{0:T(256)(128)(2,1)S(1)} %pad.9.clone, ...), kind=kLoop, calls=%fused_computation.25 | loop fusion | flops 6684672 | bytes 8716424 | tf_op jit(solution)/shard_map/concatenate | solution.py:48
  134.0 4.0 %gather_fusion.6 = bf16[68,128,128]{2,1,0:T(8,128)(2,1)} fusion(bf16[68,128,128]{2,1,0:T(8,128)(2,1)} %get-tuple-element.232, s32[1024]{0:T(1024)S(1)} %pad_clamp_fusion.4), kind=kCustom, calls=%fused_computation.6 | custom fusion | bytes 4456720 | tf_op jit(solution)/shard_map/gather | solution.py:57
  138.1 18.0 %while.24 = (s32[]{:T(128)}, f32[128,8]{0,1:T(8,128)S(1)}, s32[]{:T(128)}, s32[68,128]{1,0:T(8,128)}, bf16[68,128,128]{2,1,0:T(8,128)(2,1)}, /*index=5*/bf16[128...) while((s32[]{:T(128)}, f32[128,8]{0,1:T(8,128)S(1)}, s32[]{:T(128)}, ...), condition=%wide.region_8.9_spmd.clone, body=%wide.region_6.8_spmd.clone.sunk | while | flops 135856128 | bytes 809115 | solution.py:86
  138.1 0.9 constant_dynamic-slice_fusion.6
  140.3 0.9 constant_dynamic-slice_fusion.6
  142.6 0.9 constant_dynamic-slice_fusion.6
  144.8 0.9 constant_dynamic-slice_fusion.6
  147.1 0.9 constant_dynamic-slice_fusion.6
  149.3 0.9 constant_dynamic-slice_fusion.6
  151.6 0.9 constant_dynamic-slice_fusion.6
  153.8 0.9 constant_dynamic-slice_fusion.6
  156.0 4.0 %gather_fusion.9 = bf16[68,128,128]{2,1,0:T(8,128)(2,1)} fusion(bf16[68,128,128]{2,1,0:T(8,128)(2,1)} %get-tuple-element.231, s32[1024]{0:T(1024)S(1)} %pad_clamp_fusion.4), kind=kCustom, calls=%fused_computation.9 | custom fusion | bytes 4456720 | tf_op jit(solution)/shard_map/gather | solution.py:57
  160.1 25.0 %while.25 = (s32[]{:T(128)}, f32[128,8,128]{2,0,1:T(8,128)S(1)}, f32[128,8]{0,1:T(8,128)S(1)}, s32[]{:T(128)}, s32[68,128]{1,0:T(8,128)}, /*index=5*/bf16[68,128...) while((s32[]{:T(128)}, f32[128,8,128]{2,0,1:T(8,128)S(1)}, ...), condition=%wide.region_11.12_spmd.clone, body=%wide.region_9.11_spmd.clone.sunk | while | flops 271253504 | bytes 4352179 | solution.py:113
  160.1 1.0 constant_dynamic-slice_fusion.7
  162.0 0.7 fusion.44
  163.3 1.0 constant_dynamic-slice_fusion.7
  166.4 1.0 constant_dynamic-slice_fusion.7
  168.2 0.7 fusion.44
  169.5 1.0 constant_dynamic-slice_fusion.7
  171.4 0.7 fusion.44
  172.6 1.0 constant_dynamic-slice_fusion.7
  174.5 0.7 fusion.44
  175.8 1.0 constant_dynamic-slice_fusion.7
  177.6 0.7 fusion.44
  178.9 1.0 constant_dynamic-slice_fusion.7
  180.7 0.7 fusion.44
  182.0 1.0 constant_dynamic-slice_fusion.7
  183.9 0.7 fusion.44
  186.4 2.1 reduce.2
  188.7 25.4 %all_to_all.30 = bf16[16,2,4096]{2,1,0:T(2,128)(2,1)S(1)} all-to-all(bf16[16,2,4096]{2,1,0:T(2,128)(2,1)S(1)} %reshape.664), channel_id=1, replica_groups=mesh['req'=32,'tok'=16] {'tok'}, dimensions={0} | all-to-all | bytes 524288 | tf_op jit(solution)/shard_map/all_to_all | solution.py:228
  214.4 0.8 copy.39
  (133 shorter events, 29.4 us)
Async XLA Ops:
  0.6 25.3 %copy-start = (bf16[64,128,128]{2,1,0:T(8,128)(2,1)S(1)}, bf16[64,128,128]{2,1,0:T(8,128)(2,1)}, u32[]{:S(2)}) copy-start(bf16[64,128,128]{2,1,0:T(8,128)(2,1)} %param.14) | copy-start | bytes 6291460
  0.6 19.1 %copy-start.1 = (s32[128]{0:T(128)S(1)}, s32[128]{0:T(128)}, u32[]{:S(2)}) copy-start(s32[128]{0:T(128)} %param.16) | copy-start | bytes 1540
  0.7 22.2 %copy-start.3 = (s32[128,32,2]{0,2,1:T(2,128)S(1)}, s32[128,32,2]{0,2,1:T(2,128)}, u32[]{:S(2)}) copy-start(s32[128,32,2]{0,2,1:T(2,128)} %param.17) | copy-start | bytes 98308
  4.5 33.1 %all-to-all-start.1 = ((bf16[16,8,1024]{2,1,0:T(8,128)(2,1)}), bf16[16,8,1024]{2,1,0:T(8,128)(2,1)S(1)}, u32[]{:S(2)}, u32[]{:S(2)}) async-start(bf16[16,8,1024]{2,1,0:T(8,128)(2,1)} %bitcast.14), calls=%async_computation.1 | async-start | bytes 524288 | tf_op jit(solution)/shard_map/all_to_all | solution.py:145
  37.6 22.9 %all-to-all-start = ((bf16[32,128,128]{2,1,0:T(8,128)(2,1)}), bf16[32,128,128]{2,1,0:T(8,128)(2,1)}, u32[]{:S(2)}, u32[]{:S(2)}) async-start(bf16[32,128,128]{2,1,0:T(8,128)(2,1)} %gather_fusion.5), calls=%async_computation | async-start | bytes 2097152 | tf_op jit(solution)/shard_map/all_to_all | solution.py:175
  48.4 5.5 %copy-start.4 = (bf16[4,4,8,128]{3,2,1,0:T(8,128)(2,1)S(1)}, bf16[4,4,8,128]{3,2,1,0:T(8,128)(2,1)}, u32[]{:S(2)}) copy-start(bf16[4,4,8,128]{3,2,1,0:T(8,128)(2,1)} %param.12) | copy-start | bytes 98308
  60.5 69.8 %all-to-all-start.2 = ((bf16[32,128,128]{2,1,0:T(8,128)(2,1)}), bf16[32,128,128]{2,1,0:T(8,128)(2,1)}, u32[]{:S(2)}, u32[]{:S(2)}) async-start(bf16[32,128,128]{2,1,0:T(8,128)(2,1)} %gather_fusion.8), calls=%async_computation.2 | async-start | bytes 2097152 | tf_op jit(solution)/shard_map/all_to_all | solution.py:176
  68.1 65.9 %copy-start.2 = (bf16[4,4,8,128]{3,2,1,0:T(8,128)(2,1)}, bf16[4,4,8,128]{3,2,1,0:T(8,128)(2,1)S(1)}, u32[]{:S(2)}) copy-start(bf16[4,4,8,128]{3,2,1,0:T(8,128)(2,1)S(1)} %pad_maximum_fusion.1) | copy-start | bytes 98308
where the time goes:
time: 217 us; the launch traced here: 215 us
  blocking collectives  87.4 us (40%)
  local copies, waits for them, and re-layouts  52.8 us (24%)
  starting transfers between devices  30.2 us (14%)
  other arithmetic  16.3 us (8%)
  matrix products  13.5 us (6%)
  waiting for transfers between devices  10 us (5%)
  between operations  4.27 us (2%)
    all_gather x1, blocking collectives, per_device(): lax.all_gather(values, 'tok', axis=2, tiled=True)  32.4 us
    all_gather x1, blocking collectives, per_device(): lax.all_gather(new_keys, 'tok', axis=2, tiled=True)  29.6 us
    all_to_all x1, blocking collectives, per_device(): lax.all_to_all(attended, 'tok', split_axis=1, concat_axis=0, tiled=True)  25.4 us
    all_to_all x1, starting transfers between devices, per_device(): lax.all_to_all(query_rotated.reshape(member_count, token_slice, query_wid...  15.2 us
    all_to_all x1, waiting for transfers between devices, per_device(): lax.all_to_all(query_rotated.reshape(member_count, token_slice, query_wid...  10 us
    dot_general x16, matrix products, block_scores(): jnp.einsum('qgd,kd->qgk', rotated, key_block, preferred_element_type=jnp....  9.24 us
    dynamic_slice x8, local copies, waits for them, and re-layouts, weighted_one_block(): lax.dynamic_slice_in_dim(value_pages, block_number * block_pages, block_p...  7.95 us
    all_to_all x1, starting transfers between devices, per_device(): lax.all_to_all(outgoing_keys, 'req', split_axis=0, concat_axis=0, tiled=T...  7.54 us
  transfers between devices with their start and end apart: 3, of which 1 were waited for; matrix products, arithmetic and copies ran while one was open for 9% of the time, Pallas kernels for 0%

commit v1 on v0

v1 whole, which is shorter than its diff:
```python
import functools

import jax
import jax.numpy as jnp
import numpy as np
from jax import lax
from jax.experimental import pallas as pl
from jax.experimental.pallas import tpu as pltpu
from jax.sharding import PartitionSpec as P

THETA = 5000000.0
NEGATIVE = -1e30
MESH = pl.DeviceIdType.MESH
LOG2E = 1.4426950408889634


def exchange_kernel(
    sizes,
    table_ref,
    len_ref,
    freq_ref,
    q_ref,
    k_ref,
    v_ref,
    kpool_ref,
    vpool_ref,
    rows_out,
    pages_out,
    newk_out,
    pool_k,
    pool_v,
    send_pages,
    send_rows,
    cos_ref,
    sin_ref,
    pool_sem,
    own_sem,
    row_send,
    row_recv,
    page_send,
    page_recv,
):
    n_req, n_tok, lanes, heads, toks, group, dim = sizes
    g = lax.axis_index("req")
    z = lax.axis_index("tok")
    lane = z // heads
    pool_copies = [
        pltpu.make_async_copy(kpool_ref, pool_k, pool_sem.at[0]),
        pltpu.make_async_copy(vpool_ref, pool_v, pool_sem.at[1]),
    ]
    for c in pool_copies:
        c.start()

    barrier = pltpu.get_barrier_semaphore()

    @pl.loop(1, n_tok)
    def _(d):
        pl.semaphore_signal(
            barrier, inc=1, device_id=(g, lax.rem(z + d, n_tok)), device_id_type=MESH
        )

    @pl.loop(1, n_req)
    def _(d):
        pl.semaphore_signal(
            barrier, inc=1, device_id=(lax.rem(g + d, n_req), z), device_id_type=MESH
        )

    steps = lax.broadcasted_iota(jnp.int32, (toks, dim), 0)
    cols = lax.broadcasted_iota(jnp.int32, (toks, dim), 1)
    for r in range(lanes):
        first = len_ref[g * lanes + r] + z * toks
        angle = (first + steps).astype(jnp.float32) * freq_ref[0:1, :]
        cos_ref[r] = jnp.cos(angle)
        sine = jnp.sin(angle)
        sin_ref[r] = jnp.where(cols < dim // 2, -sine, sine)

    @pl.loop(0, n_tok)
    def _(m):
        r = m // heads
        cosine = cos_ref[r]
        sine = sin_ref[r]

        def rotate(x):
            return (x * cosine + pltpu.roll(x, dim // 2, 1) * sine).astype(jnp.bfloat16)

        for j in range(group):
            x = q_ref[m, :, j * dim : (j + 1) * dim].astype(jnp.float32)
            send_rows[m, :, j * dim : (j + 1) * dim] = rotate(x)
        key = rotate(k_ref[m].astype(jnp.float32))
        send_rows[m, :, group * dim : (group + 1) * dim] = key
        newk_out[m] = key
        send_rows[m, :, (group + 1) * dim : (group + 2) * dim] = v_ref[m]

    own = pltpu.make_async_copy(send_rows.at[z], rows_out.at[z], own_sem)
    own.start()
    pl.semaphore_wait(barrier, n_tok + n_req - 2)

    def row_copy(d):
        t = lax.rem(z + d, n_tok)
        return pltpu.make_async_remote_copy(
            src_ref=send_rows.at[t],
            dst_ref=rows_out.at[z],
            send_sem=row_send.at[d],
            recv_sem=row_recv.at[d],
            device_id=(g, t),
            device_id_type=MESH,
        )

    @pl.loop(1, n_tok)
    def _(d):
        row_copy(d).start()

    for c in pool_copies:
        c.wait()

    @pl.loop(1, n_req)
    def _(d):
        j = lax.rem(g + d, n_req)
        p = n_req - 1 - d
        slot = table_ref[p, 1, j * lanes + lane]
        slot = jnp.clip(slot, 0, pool_k.shape[0] - 1)
        send_pages[p, 0] = pool_k[slot]
        send_pages[p, 1] = pool_v[slot]

    def page_copy(p):
        j = lax.rem(g + n_req - 1 - p, n_req)
        return pltpu.make_async_remote_copy(
            src_ref=send_pages.at[p],
            dst_ref=pages_out.at[p],
            send_sem=page_send.at[p],
            recv_sem=page_recv.at[p],
            device_id=(j, z),
            device_id_type=MESH,
        )

    @pl.loop(0, n_req - 1)
    def _(p):
        page_copy(p).start()

    own.wait()

    @pl.loop(1, n_tok)
    def _(d):
        s = lax.rem(z + n_tok - d, n_tok)
        c = pltpu.make_async_remote_copy(
            src_ref=send_rows.at[s],
            dst_ref=rows_out.at[s],
            send_sem=row_send.at[d],
            recv_sem=row_recv.at[d],
            device_id=(g, lax.rem(z + d, n_tok)),
            device_id_type=MESH,
        )
        c.wait_send()
        c.wait_recv()

    @pl.loop(0, n_req - 1)
    def _(p):
        c = page_copy(p)
        c.wait_send()
        c.wait_recv()


def attend_block(q_ref, keys, values, m_ref, l_ref, acc_ref, factor, chunk, mask=None):
    rows = q_ref.shape[0]
    n_keys = keys.shape[0]
    lane_blocks = n_keys // 128
    for start in range(0, rows, chunk):
        at = slice(start, start + chunk)
        s = (
            lax.dot_general(
                q_ref[at], keys, (((1,), (1,)), ((), ())), preferred_element_type=jnp.float32
            )
            * factor
        )
        if mask is not None:
            s = jnp.where(mask, s, NEGATIVE)
        m_old = m_ref[at]
        m_new = jnp.maximum(m_old, jnp.max(s, axis=1, keepdims=True))
        m_ref[at] = m_new
        alpha = jnp.exp2(m_old - m_new)
        pieces = [jnp.exp2(s[:, i * 128 : (i + 1) * 128] - m_new) for i in range(lane_blocks)]
        total = pieces[0]
        for piece in pieces[1:]:
            total = total + piece
        l_ref[at] = l_ref[at] * alpha + total
        weights = jnp.concatenate([piece.astype(jnp.bfloat16) for piece in pieces], axis=1)
        acc_ref[at] = acc_ref[at] * alpha + jnp.dot(
            weights, values, preferred_element_type=jnp.float32
        )


def attend_kernel(
    sizes,
    table_ref,
    len_ref,
    rows_ref,
    pages_ref,
    kpool_ref,
    vpool_ref,
    out_ref,
    key_buf,
    value_buf,
    q_buf,
    m_ref,
    l_ref,
    acc_ref,
    sems,
):
    n_req, n_tok, lanes, heads, toks, group, dim = sizes
    page = key_buf.shape[1]
    limit = key_buf.shape[0]
    g = lax.axis_index("req")
    z = lax.axis_index("tok")
    request = g * lanes + z // heads
    count = len_ref[request] // page
    remote = table_ref[0, 0, request] != g

    def fetches(p):
        slot = jnp.clip(table_ref[p, 1, request], 0, kpool_ref.shape[0] - 1)
        return slot

    @pl.loop(0, count)
    def _(p):
        far = jnp.logical_and(remote, p < n_req - 1)

        @pl.when(far)
        def _():
            pltpu.make_async_copy(pages_ref.at[p, 0], key_buf.at[p], sems.at[0, p]).start()
            pltpu.make_async_copy(pages_ref.at[p, 1], value_buf.at[p], sems.at[1, p]).start()

        @pl.when(jnp.logical_not(far))
        def _():
            slot = fetches(p)
            pltpu.make_async_copy(kpool_ref.at[slot], key_buf.at[p], sems.at[0, p]).start()
            pltpu.make_async_copy(vpool_ref.at[slot], value_buf.at[p], sems.at[1, p]).start()

    def wait(p):
        pltpu.make_async_copy(pages_ref.at[0, 0], key_buf.at[p], sems.at[0, p]).wait()
        pltpu.make_async_copy(pages_ref.at[0, 1], value_buf.at[p], sems.at[1, p]).wait()

    added = n_tok * toks
    for j in range(group):
        x = rows_ref[:, :, j * dim : (j + 1) * dim].astype(jnp.float32)
        q_buf[j * added : (j + 1) * added] = x.reshape(added, dim).astype(jnp.bfloat16)
    m_ref[...] = jnp.full_like(m_ref, NEGATIVE)
    l_ref[...] = jnp.zeros_like(l_ref)
    acc_ref[...] = jnp.zeros_like(acc_ref)
    factor = dim ** (-0.5) * LOG2E
    run = functools.partial(
        attend_block, q_buf, m_ref=m_ref, l_ref=l_ref, acc_ref=acc_ref, factor=factor
    )

    def fresh(j):
        x = rows_ref[:, :, j * dim : (j + 1) * dim].astype(jnp.float32)
        return x.reshape(added, dim).astype(jnp.bfloat16)

    token = lax.broadcasted_iota(jnp.int32, (added, added), 0)
    place = lax.broadcasted_iota(jnp.int32, (added, added), 1)
    run(fresh(group), fresh(group + 1), chunk=added, mask=place <= token)

    step = 4

    @pl.loop(0, count // step)
    def _(b):
        for i in range(step):
            wait(b * step + i)
        run(
            key_buf[pl.ds(b * step, step)].reshape(step * page, dim),
            value_buf[pl.ds(b * step, step)].reshape(step * page, dim),
            chunk=256,
        )

    @pl.loop(count // step * step, count)
    def _(p):
        wait(p)
        run(key_buf[p], value_buf[p], chunk=256)

    for j in range(group):
        at = slice(j * added, (j + 1) * added)
        total = jnp.sum(l_ref[at], axis=1, keepdims=True)
        x = acc_ref[at] / total
        out_ref[:, :, j * dim : (j + 1) * dim] = x.reshape(n_tok, toks, dim).astype(jnp.bfloat16)


def return_kernel(sizes, in_ref, out_ref, own_sem, send_sem, recv_sem):
    n_req, n_tok, lanes, heads, toks, group, dim = sizes
    g = lax.axis_index("req")
    z = lax.axis_index("tok")
    own = pltpu.make_async_copy(in_ref.at[z], out_ref.at[z], own_sem)
    own.start()
    barrier = pltpu.get_barrier_semaphore()

    @pl.loop(1, n_tok)
    def _(d):
        pl.semaphore_signal(
            barrier, inc=1, device_id=(g, lax.rem(z + d, n_tok)), device_id_type=MESH
        )

    pl.semaphore_wait(barrier, n_tok - 1)

    @pl.loop(1, n_tok)
    def _(d):
        t = lax.rem(z + d, n_tok)
        pltpu.make_async_remote_copy(
            src_ref=in_ref.at[t],
            dst_ref=out_ref.at[z],
            send_sem=send_sem.at[d],
            recv_sem=recv_sem.at[d],
            device_id=(g, t),
            device_id_type=MESH,
        ).start()

    own.wait()

    @pl.loop(1, n_tok)
    def _(d):
        s = lax.rem(z + n_tok - d, n_tok)
        c = pltpu.make_async_remote_copy(
            src_ref=in_ref.at[s],
            dst_ref=out_ref.at[s],
            send_sem=send_sem.at[d],
            recv_sem=recv_sem.at[d],
            device_id=(g, lax.rem(z + d, n_tok)),
            device_id_type=MESH,
        )
        c.wait_send()
        c.wait_recv()


def per_device(queries, keys, values, key_cache_pool, value_cache_pool, cached_len, page_table):
    n_req = lax.axis_size("req")
    n_tok = lax.axis_size("tok")
    lanes, heads, toks, width = queries.shape
    dim = keys.shape[-1]
    group = width // dim
    slots, page = key_cache_pool.shape[:2]
    limit = page_table.shape[1]
    sizes = (n_req, n_tok, lanes, heads, toks, group, dim)
    table = jnp.transpose(page_table, (1, 2, 0))
    half = np.arange(dim // 2, dtype=np.float32)
    inverse = np.float32(THETA) ** (-(half * np.float32(2.0) / np.float32(dim)))
    freq = jnp.asarray(np.tile(inverse.astype(np.float32), 2).reshape(1, dim))
    smem = pl.BlockSpec(memory_space=pltpu.SMEM)
    vmem = pl.BlockSpec(memory_space=pltpu.VMEM)
    hbm = pl.BlockSpec(memory_space=pl.ANY)
    bf16 = jnp.bfloat16
    rows, pages, new_keys = pl.pallas_call(
        functools.partial(exchange_kernel, sizes),
        out_shape=(
            jax.ShapeDtypeStruct((n_tok, toks, width + 2 * dim), bf16),
            jax.ShapeDtypeStruct((n_req - 1, 2, page, dim), bf16),
            jax.ShapeDtypeStruct((n_tok, toks, dim), bf16),
        ),
        in_specs=[smem, smem, vmem, vmem, vmem, vmem, hbm, hbm],
        out_specs=(hbm, hbm, vmem),
        scratch_shapes=[
            pltpu.VMEM((slots, page, dim), bf16),
            pltpu.VMEM((slots, page, dim), bf16),
            pltpu.VMEM((n_req - 1, 2, page, dim), bf16),
            pltpu.VMEM((n_tok, toks, width + 2 * dim), bf16),
            pltpu.VMEM((lanes, toks, dim), jnp.float32),
            pltpu.VMEM((lanes, toks, dim), jnp.float32),
            pltpu.SemaphoreType.DMA((2,)),
            pltpu.SemaphoreType.DMA,
            pltpu.SemaphoreType.DMA((n_tok,)),
            pltpu.SemaphoreType.DMA((n_tok,)),
            pltpu.SemaphoreType.DMA((n_req - 1,)),
            pltpu.SemaphoreType.DMA((n_req - 1,)),
        ],
        compiler_params=pltpu.CompilerParams(collective_id=0, has_side_effects=True),
        name="exchange_in",
    )(
        table,
        cached_len,
        freq,
        queries.reshape(n_tok, toks, width),
        keys.reshape(n_tok, toks, dim),
        values.reshape(n_tok, toks, dim),
        key_cache_pool,
        value_cache_pool,
    )
    added = n_tok * toks
    attended = pl.pallas_call(
        functools.partial(attend_kernel, sizes),
        out_shape=jax.ShapeDtypeStruct((n_tok, toks, width), bf16),
        in_specs=[smem, smem, vmem, hbm, hbm, hbm],
        out_specs=vmem,
        scratch_shapes=[
            pltpu.VMEM((limit, page, dim), bf16),
            pltpu.VMEM((limit, page, dim), bf16),
            pltpu.VMEM((added * group, dim), bf16),
            pltpu.VMEM((added * group, dim), jnp.float32),
            pltpu.VMEM((added * group, dim), jnp.float32),
            pltpu.VMEM((added * group, dim), jnp.float32),
            pltpu.SemaphoreType.DMA((2, limit)),
        ],
        name="attend",
    )(table, cached_len, rows, pages, key_cache_pool, value_cache_pool)
    returned = pl.pallas_call(
        functools.partial(return_kernel, sizes),
        out_shape=jax.ShapeDtypeStruct((n_tok, toks, width), bf16),
        in_specs=[vmem],
        out_specs=vmem,
        scratch_shapes=[
            pltpu.SemaphoreType.DMA,
            pltpu.SemaphoreType.DMA((n_tok,)),
            pltpu.SemaphoreType.DMA((n_tok,)),
        ],
        compiler_params=pltpu.CompilerParams(collective_id=1, has_side_effects=True),
        name="exchange_out",
    )(attended)
    return (
        returned.reshape(lanes, heads, toks, width),
        new_keys.reshape(lanes, heads, toks, dim),
    )


def solution(mesh):
    placed = (
        P("req", None, "tok", None),
        P("req", None, "tok", None),
        P("req", None, "tok", None),
        P("req", None, "tok"),
        P("req", None, "tok"),
        P(),
        P(),
    )
    return jax.shard_map(
        per_device,
        mesh=mesh,
        in_specs=placed,
        out_specs=(P("req", None, "tok", None), P("req", None, "tok", None)),
        check_vma=False,
    )
```

time: 217 us -> 92.2 us (0.42)
  the two profiles are of different devices: /device:TPU:44 before, /device:TPU:8 now
where the time goes in v1:
time: 92.2 us; the launch traced here: 91.9 us
  Pallas kernels  88.9 us (96%)
  local copies, waits for them, and re-layouts  2.29 us (2%)
    pallas_call x1, Pallas kernels, per_device(): pl.pallas_call(functools.partial(exchange_kernel, sizes), out_shape=(jax....  48.4 us
    pallas_call x1, Pallas kernels, per_device(): pl.pallas_call(functools.partial(return_kernel, sizes), out_shape=jax.Sha...  24.5 us
    pallas_call x1, Pallas kernels, per_device(): pl.pallas_call(functools.partial(attend_kernel, sizes), out_shape=jax.Sha...  16 us
    unnamed x4, local copies, waits for them, and re-layouts  2.29 us

profile of v1, /device:TPU:8, one launch (start us, length us, event | category | flops | bytes accessed | tf_op | source)
XLA Modules:
  0.0 91.9 jit_solution(10780047033908905965)
XLA Ops:
  0.6 48.4 %exchange_in.1 = (bf16[16,8,1280]{2,1,0:T(8,128)(2,1)}, bf16[31,2,128,128]{3,2,1,0:T(8,128)(2,1)}, bf16[16,8,128]{2,1,0:T(8,128)(2,1)}) custom-call(s32[32,2,128]{2,1,0:T(2,128)} %bitcast.8, s32[128]{0:T(128)} %len_ref.3, f32[1,128]{1,0:T(1,128)} %constant.2.clone.freq_ref, bf16[16,8,1024]{2,1,0:T(8,128)(2,1)} %bitcast.7, bf16[16,8,128]{2,1,0:T(8,128)(2,1)} %bitcast.10, ...), custom_call_target="tpu_custom_call" | custom-call | tf_op jit(solution)/shard_map/exchange_in/pallas_call | solution.py:347
  49.1 0.0 copy-start
  49.1 16.0 %attend.1.in_ref = bf16[16,8,1024]{2,1,0:T(8,128)(2,1)} custom-call(s32[32,2,128]{2,1,0:T(2,128)} %bitcast.9, s32[128]{0:T(128)} %len_ref.3, bf16[16,8,1280]{2,1,0:T(8,128)(2,1)} %get-tuple-element.5.rows_ref, bf16[31,2,128,128]{3,2,1,0:T(8,128)(2,1)} %get-tuple-element.6.pages_ref, bf16[64,128,128]{2,1,0:T(8,128)(2,1)} %kpool_ref.3, ...), custom_call_target="tpu_custom_call" | custom-call | tf_op jit(solution)/shard_map/attend/pallas_call | solution.py:383
  65.1 24.5 %exchange_out.1 = bf16[16,8,1024]{2,1,0:T(8,128)(2,1)} custom-call(bf16[16,8,1024]{2,1,0:T(8,128)(2,1)} %attend.1.in_ref), custom_call_target="tpu_custom_call" | custom-call | tf_op jit(solution)/shard_map/exchange_out/pallas_call | solution.py:399
  89.6 1.7 %copy.12 = bf16[4,4,8,1024]{3,2,1,0:T(8,128)(2,1)} copy(bf16[4,4,8,1024]{3,2,1,0:T(8,128)(2,1)} %bitcast.6) | data formatting | bytes 524288
  91.3 0.0 copy-done
  91.3 0.6 copy.13
Async XLA Ops:
  49.1 42.2 %copy-start = (bf16[16,8,128]{2,1,0:T(8,128)(2,1)S(1)}, bf16[16,8,128]{2,1,0:T(8,128)(2,1)}, u32[]{:S(2)}) copy-start(bf16[16,8,128]{2,1,0:T(8,128)(2,1)} %get-tuple-element.7) | copy-start | bytes 98308

commit v2 on v1

v2 whole, which is shorter than its diff:
```python
import functools

import jax
import jax.numpy as jnp
import numpy as np
from jax import lax
from jax.experimental import pallas as pl
from jax.experimental.pallas import tpu as pltpu
from jax.sharding import PartitionSpec as P

THETA = 5000000.0
NEGATIVE = -1e30
MESH = pl.DeviceIdType.MESH
LOG2E = 1.4426950408889634
RING_Y, RING_X, CORES = 4, 4, 2
STEP = 4
CHUNK = 512


def ring_distance(d, n):
    return min(d % n, n - d % n)


PARTNERS = sorted(
    [
        (dy, dx, dc)
        for dy in range(RING_Y)
        for dx in range(RING_X)
        for dc in range(CORES)
        if (dy, dx, dc) != (0, 0, 0)
    ],
    key=lambda o: -(ring_distance(o[0], RING_Y) + ring_distance(o[1], RING_X)),
)


def tok_order(n):
    return sorted(range(1, n), key=lambda d: -ring_distance(d, n))


def partner(g, offset, sign):
    dy, dx, dc = offset
    c = lax.rem(g, CORES)
    x = lax.rem(g // CORES, RING_X)
    y = g // (CORES * RING_X)
    y = lax.rem(y + sign * dy + RING_Y, RING_Y)
    x = lax.rem(x + sign * dx + RING_X, RING_X)
    c = lax.rem(c + dc, CORES)
    return (y * RING_X + x) * CORES + c


def layer_kernel(
    sizes,
    table_ref,
    len_ref,
    freq_ref,
    q_hbm,
    k_hbm,
    v_hbm,
    kpool_ref,
    vpool_ref,
    out_ref,
    newk_out,
    q_in,
    k_in,
    v_in,
    newk,
    pool_k,
    pool_v,
    send_pages,
    recv_pages,
    send_rows,
    recv_rows,
    out_rows,
    cos_ref,
    sin_ref,
    page_ids,
    q_buf,
    fill,
    key_blk,
    value_t,
    s_buf,
    m_ref,
    m_old_ref,
    alpha_ref,
    l_ref,
    acc_ref,
    in_sem,
    pool_sem,
    newk_sem,
    own_sem,
    row_send,
    row_recv,
    page_send,
    page_recv,
    out_send,
    out_recv,
):
    n_req, n_tok, lanes, heads, toks, group, dim = sizes
    added = n_tok * toks
    rows = added * group
    page = pool_k.shape[1]
    n_far = n_req - 1
    factor = dim ** (-0.5) * LOG2E
    g = lax.axis_index("req")
    z = lax.axis_index("tok")
    lane = z // heads
    request = g * lanes + lane

    in_copies = [
        pltpu.make_async_copy(src, dst, in_sem.at[i])
        for i, (src, dst) in enumerate(((q_hbm, q_in), (k_hbm, k_in), (v_hbm, v_in)))
    ]
    pool_copies = [
        pltpu.make_async_copy(kpool_ref, pool_k, pool_sem.at[0]),
        pltpu.make_async_copy(vpool_ref, pool_v, pool_sem.at[1]),
    ]
    for c in in_copies:
        c.start()
    for c in pool_copies:
        c.start()

    barrier = pltpu.get_barrier_semaphore()
    z_order = tok_order(n_tok)
    for d in z_order:
        pl.semaphore_signal(
            barrier, inc=1, device_id=(g, lax.rem(z + d, n_tok)), device_id_type=MESH
        )
    for offset in PARTNERS:
        pl.semaphore_signal(
            barrier, inc=1, device_id=(partner(g, offset, 1), z), device_id_type=MESH
        )

    for k, offset in enumerate(PARTNERS):
        page_ids[k] = lax.rem(partner(g, offset, -1) + n_req - g + n_req - 1, n_req)
    page_ids[n_far] = n_req - 1

    steps = lax.broadcasted_iota(jnp.int32, (toks, dim), 0)
    cols = lax.broadcasted_iota(jnp.int32, (toks, dim), 1)
    for r in range(lanes):
        first = len_ref[g * lanes + r] + z * toks
        angle = (first + steps).astype(jnp.float32) * freq_ref[0:1, :]
        cos_ref[r] = jnp.cos(angle)
        sine = jnp.sin(angle)
        sin_ref[r] = jnp.where(cols < dim // 2, -sine, sine)

    for c in in_copies:
        c.wait()

    @pl.loop(0, n_tok)
    def _(m):
        r = m // heads
        cosine = cos_ref[r]
        sine = sin_ref[r]

        def rotate(x):
            return (x * cosine + pltpu.roll(x, dim // 2, 1) * sine).astype(jnp.bfloat16)

        for j in range(group):
            x = q_in[m, :, j * dim : (j + 1) * dim].astype(jnp.float32)
            send_rows[m, :, j * dim : (j + 1) * dim] = rotate(x)
        key = rotate(k_in[m].astype(jnp.float32))
        send_rows[m, :, group * dim : (group + 1) * dim] = key
        newk[m] = key
        send_rows[m, :, (group + 1) * dim : (group + 2) * dim] = v_in[m]

    newk_copy = pltpu.make_async_copy(newk, newk_out, newk_sem)
    newk_copy.start()
    for c in pool_copies:
        c.wait()

    def slot_of(p, r):
        return jnp.clip(table_ref[p, 1, r], 0, pool_k.shape[0] - 1)

    for k, offset in enumerate(PARTNERS):
        j = partner(g, offset, 1)
        slot = slot_of(lax.rem(g + n_req - j + n_req - 1, n_req), j * lanes + lane)
        send_pages[k, 0] = pool_k[slot]
        send_pages[k, 1] = pool_v[slot]

    recv_rows[z] = send_rows[z]
    pl.semaphore_wait(barrier, n_tok + n_req - 2)

    def row_copy(d):
        t = lax.rem(z + d, n_tok)
        return pltpu.make_async_remote_copy(
            src_ref=send_rows.at[t],
            dst_ref=recv_rows.at[z],
            send_sem=row_send.at[d],
            recv_sem=row_recv.at[d],
            device_id=(g, t),
            device_id_type=MESH,
        )

    def page_copy(k):
        return pltpu.make_async_remote_copy(
            src_ref=send_pages.at[k],
            dst_ref=recv_pages.at[k],
            send_sem=page_send.at[k],
            recv_sem=page_recv.at[k],
            device_id=(partner(g, PARTNERS[k], 1), z),
            device_id_type=MESH,
        )

    for d in z_order:
        row_copy(d).start()
    for k in range(n_far):
        page_copy(k).start()

    def wait_row(d):
        s = lax.rem(z + n_tok - d, n_tok)
        pltpu.make_async_remote_copy(
            src_ref=send_rows.at[s],
            dst_ref=recv_rows.at[s],
            send_sem=row_send.at[d],
            recv_sem=row_recv.at[d],
            device_id=(g, lax.rem(z + d, n_tok)),
            device_id_type=MESH,
        ).wait_recv()

    def wait_page(k):
        pltpu.make_async_remote_copy(
            src_ref=send_pages.at[k],
            dst_ref=recv_pages.at[k],
            send_sem=page_send.at[k],
            recv_sem=page_recv.at[k],
            device_id=(lax.rem(g + 1, n_req), z),
            device_id_type=MESH,
        ).wait_recv()

    count = len_ref[request] // page
    remote = table_ref[0, 0, request] != g

    @pl.loop(1, n_tok)
    def _(d):
        wait_row(d)

    def columns(j):
        x = recv_rows[:, :, j * dim : (j + 1) * dim].astype(jnp.float32)
        return x.reshape(added, dim)

    for j in range(group):
        q_buf[j * added : (j + 1) * added] = columns(j).astype(jnp.bfloat16)
    fresh_k = columns(group)
    fresh_v = columns(group + 1)
    fill[...] = jnp.broadcast_to(fresh_k[0:1, :], (page, dim)).astype(jnp.bfloat16)

    m_ref[...] = jnp.full_like(m_ref, NEGATIVE)
    l_ref[...] = jnp.zeros_like(l_ref)
    acc_ref[...] = jnp.zeros_like(acc_ref)

    def put_page(slot, i, live, keys, values):
        at = slice(i * page, (i + 1) * page)
        key_blk[slot, at] = jnp.where(live, keys, fill[...])
        value_t[slot, :, at] = jnp.where(live, values, jnp.zeros_like(values)).T

    def live_page(k):
        return page_ids[k] < count

    def stage(first, n, slot):
        for i in range(n):
            k = first + i
            wait_page(k)
            at = slot_of(page_ids[k], request)
            keys = jnp.where(remote, recv_pages[k, 0], pool_k[at])
            values = jnp.where(remote, recv_pages[k, 1], pool_v[at])
            put_page(slot, i, live_page(k), keys, values)

    chunks = range(0, rows, CHUNK)

    def score(slot, n, c0, mask=None):
        at = slice(c0, c0 + CHUNK)
        s = lax.dot_general(
            key_blk[slot, : n * page],
            q_buf[at],
            (((1,), (1,)), ((), ())),
            preferred_element_type=jnp.float32,
        )
        if mask is not None:
            s = jnp.where(mask, s, NEGATIVE)
        s_buf[slot, : n * page, at] = s
        m_old = m_ref[:, at]
        m_new = jnp.maximum(m_old, jnp.max(s, axis=0, keepdims=True))
        m_ref[:, at] = m_new
        m_old_ref[slot, :, at] = m_new
        alpha_ref[slot, :, at] = jnp.exp2((m_old - m_new) * factor)

    def gather(slot, n, c0, lives):
        at = slice(c0, c0 + CHUNK)
        weights = jnp.exp2((s_buf[slot, : n * page, at] - m_old_ref[slot, :, at]) * factor)
        alpha = alpha_ref[slot, :, at]
        total = l_ref[:, at] * alpha
        for i in range(n):
            part = weights[i * page : (i + 1) * page].reshape(page // 8, 8, CHUNK)
            part = jnp.sum(part, axis=0)
            if lives[i] is not None:
                part = part * lives[i].astype(jnp.float32)
            total = total + part
        l_ref[:, at] = total
        acc_ref[:, at] = acc_ref[:, at] * alpha + jnp.dot(
            value_t[slot, :, : n * page],
            weights.astype(jnp.bfloat16),
            preferred_element_type=jnp.float32,
        )

    def lives_of(first, n):
        return [live_page(first + i) for i in range(n)]

    key_blk[0, :page] = fresh_k.astype(jnp.bfloat16)
    value_t[0, :, :page] = fresh_v.T.astype(jnp.bfloat16)
    own_slot = slot_of(n_req - 1, request)
    put_page(0, 1, live_page(n_far), pool_k[own_slot], pool_v[own_slot])
    place = lax.broadcasted_iota(jnp.int32, (2 * page, CHUNK), 0)
    token = lax.rem(lax.broadcasted_iota(jnp.int32, (2 * page, CHUNK), 1), added)
    visible = jnp.logical_or(place <= token, place >= page)
    for c0 in chunks:
        score(0, 2, c0, visible)
    stage(0, STEP, 1)
    for c0 in chunks:
        score(1, STEP, c0)
        gather(0, 2, c0, [None, live_page(n_far)])

    full = n_far // STEP
    tail = n_far - full * STEP
    pairs = (full - 1) // 2

    @pl.loop(0, pairs)
    def _(b):
        for i in range(2):
            first = (2 * b + i + 1) * STEP
            stage(first, STEP, i)
            for c0 in chunks:
                score(i, STEP, c0)
                gather(1 - i, STEP, c0, lives_of(first - STEP, STEP))

    last = full * STEP
    stage(last, tail, 0)
    for c0 in chunks:
        score(0, tail, c0)
        gather(1, STEP, c0, lives_of(last - STEP, STEP))
    for c0 in chunks:
        gather(0, tail, c0, lives_of(last, tail))

    total = jnp.sum(l_ref[...], axis=0, keepdims=True)
    for j in range(group):
        at = slice(j * added, (j + 1) * added)
        x = (acc_ref[:, at] / total[:, at]).T
        out_rows[:, :, j * dim : (j + 1) * dim] = x.reshape(n_tok, toks, dim).astype(jnp.bfloat16)

    def out_copy(d):
        t = lax.rem(z + d, n_tok)
        return pltpu.make_async_remote_copy(
            src_ref=out_rows.at[t],
            dst_ref=out_ref.at[z],
            send_sem=out_send.at[d],
            recv_sem=out_recv.at[d],
            device_id=(g, t),
            device_id_type=MESH,
        )

    for d in z_order:
        out_copy(d).start()
    own = pltpu.make_async_copy(out_rows.at[z], out_ref.at[z], own_sem)
    own.start()

    @pl.loop(1, n_tok)
    def _(d):
        row_copy(d).wait_send()

    for k in range(n_far):
        page_copy(k).wait_send()
    newk_copy.wait()
    own.wait()

    @pl.loop(1, n_tok)
    def _(d):
        s = lax.rem(z + n_tok - d, n_tok)
        c = pltpu.make_async_remote_copy(
            src_ref=out_rows.at[s],
            dst_ref=out_ref.at[s],
            send_sem=out_send.at[d],
            recv_sem=out_recv.at[d],
            device_id=(g, lax.rem(z + d, n_tok)),
            device_id_type=MESH,
        )
        c.wait_send()
        c.wait_recv()


def per_device(queries, keys, values, key_cache_pool, value_cache_pool, cached_len, page_table):
    n_req = lax.axis_size("req")
    n_tok = lax.axis_size("tok")
    lanes, heads, toks, width = queries.shape
    dim = keys.shape[-1]
    group = width // dim
    slots, page = key_cache_pool.shape[:2]
    sizes = (n_req, n_tok, lanes, heads, toks, group, dim)
    rows = n_tok * toks * group
    table = jnp.transpose(page_table, (1, 2, 0))
    half = np.arange(dim // 2, dtype=np.float32)
    inverse = np.float32(THETA) ** (-(half * np.float32(2.0) / np.float32(dim)))
    freq = jnp.asarray(np.tile(inverse.astype(np.float32), 2).reshape(1, dim))
    smem = pl.BlockSpec(memory_space=pltpu.SMEM)
    vmem = pl.BlockSpec(memory_space=pltpu.VMEM)
    hbm = pl.BlockSpec(memory_space=pl.ANY)
    bf16, f32 = jnp.bfloat16, jnp.float32
    dma = pltpu.SemaphoreType.DMA
    returned, new_keys = pl.pallas_call(
        functools.partial(layer_kernel, sizes),
        out_shape=(
            jax.ShapeDtypeStruct((n_tok, toks, width), bf16),
            jax.ShapeDtypeStruct((n_tok, toks, dim), bf16),
        ),
        in_specs=[smem, smem, vmem, hbm, hbm, hbm, hbm, hbm],
        out_specs=(hbm, hbm),
        scratch_shapes=[
            pltpu.VMEM((n_tok, toks, width), bf16),
            pltpu.VMEM((n_tok, toks, dim), bf16),
            pltpu.VMEM((n_tok, toks, dim), bf16),
            pltpu.VMEM((n_tok, toks, dim), bf16),
            pltpu.VMEM((slots, page, dim), bf16),
            pltpu.VMEM((slots, page, dim), bf16),
            pltpu.VMEM((n_req - 1, 2, page, dim), bf16),
            pltpu.VMEM((n_req - 1, 2, page, dim), bf16),
            pltpu.VMEM((n_tok, toks, width + 2 * dim), bf16),
            pltpu.VMEM((n_tok, toks, width + 2 * dim), bf16),
            pltpu.VMEM((n_tok, toks, width), bf16),
            pltpu.VMEM((lanes, toks, dim), f32),
            pltpu.VMEM((lanes, toks, dim), f32),
            pltpu.SMEM((n_req,), jnp.int32),
            pltpu.VMEM((rows, dim), bf16),
            pltpu.VMEM((page, dim), bf16),
            pltpu.VMEM((2, STEP * page, dim), bf16),
            pltpu.VMEM((2, dim, STEP * page), bf16),
            pltpu.VMEM((2, STEP * page, rows), f32),
            pltpu.VMEM((1, rows), f32),
            pltpu.VMEM((2, 1, rows), f32),
            pltpu.VMEM((2, 1, rows), f32),
            pltpu.VMEM((8, rows), f32),
            pltpu.VMEM((dim, rows), f32),
            dma((3,)),
            dma((2,)),
            dma,
            dma,
            dma((n_tok,)),
            dma((n_tok,)),
            dma((n_req - 1,)),
            dma((n_req - 1,)),
            dma((n_tok,)),
            dma((n_tok,)),
        ],
        compiler_params=pltpu.CompilerParams(collective_id=0, has_side_effects=True),
        name="layer",
    )(
        table,
        cached_len,
        freq,
        queries.reshape(n_tok, toks, width),
        keys.reshape(n_tok, toks, dim),
        values.reshape(n_tok, toks, dim),
        key_cache_pool,
        value_cache_pool,
    )
    return (
        returned.reshape(lanes, heads, toks, width),
        new_keys.reshape(lanes, heads, toks, dim),
    )


def solution(mesh):
    placed = (
        P("req", None, "tok", None),
        P("req", None, "tok", None),
        P("req", None, "tok", None),
        P("req", None, "tok"),
        P("req", None, "tok"),
        P(),
        P(),
    )
    return jax.shard_map(
        per_device,
        mesh=mesh,
        in_specs=placed,
        out_specs=(P("req", None, "tok", None), P("req", None, "tok", None)),
        check_vma=False,
    )
```

time: 92.2 us -> 65.3 us (0.71)
  the two profiles are of different devices: /device:TPU:8 before, /device:TPU:4 now
where the time goes in v2:
time: 65.3 us; the launch traced here: 65 us
  Pallas kernels  61.3 us (94%)
  local copies, waits for them, and re-layouts  3.04 us (5%)
    pallas_call x1, Pallas kernels, per_device(): pl.pallas_call(functools.partial(layer_kernel, sizes), out_shape=(jax.Sha...  61.3 us
    unnamed x2, local copies, waits for them, and re-layouts  3.04 us

profile of v2, /device:TPU:4, one launch (start us, length us, event | category | flops | bytes accessed | tf_op | source)
XLA Modules:
  0.0 65.0 jit_solution(5564366266973727485)
XLA Ops:
  0.6 61.3 %layer.1 = (bf16[16,8,1024]{2,1,0:T(8,128)(2,1)}, bf16[16,8,128]{2,1,0:T(8,128)(2,1)}) custom-call(s32[32,2,128]{2,1,0:T(2,128)} %bitcast.8, s32[128]{0:T(128)} %len_ref.1, f32[1,128]{1,0:T(1,128)} %constant.2.clone.freq_ref, bf16[16,8,1024]{2,1,0:T(8,128)(2,1)} %bitcast.6, bf16[16,8,128]{2,1,0:T(8,128)(2,1)} %bitcast.9, bf16[16,8,128]{2,1,0:T(8,128)(2,1)} %bitcast.10, ...), custom_call_target="tpu_custom_call" | custom-call | tf_op jit(solution)/shard_map/layer/pallas_call | solution.py:407
  61.9 1.7 %copy.12 = bf16[4,4,8,1024]{3,2,1,0:T(8,128)(2,1)} copy(bf16[4,4,8,1024]{3,2,1,0:T(8,128)(2,1)} %bitcast.7) | data formatting | bytes 524288
  63.6 1.4 %copy.13 = bf16[4,4,8,128]{3,2,1,0:T(8,128)(2,1)} copy(bf16[4,4,8,128]{3,2,1,0:T(8,128)(2,1)} %bitcast.11) | data formatting | bytes 65536
